TPU v7x, 512 devices: a whole 4x8x8 slice. The times are simulated.
512 devices in a mesh: dp: 8 (over z), section: 4 (over x), patch: 16 (over y, core).
Axes of the slice: x: 4, y: 8, z: 8, core: 2. Of those that a mesh axis runs over, the one named last changes fastest.
Arguments:
- maps: bfloat16 [4, 8, 1536, 256], P(None, 'dp', 'patch'), may hold values from -6 to 6
- upstream: bfloat16 [4, 8, 1536, 256], P(None, 'dp', 'patch'), may hold values from -6 to 6
- weights: bfloat16 [4, 2304, 256], P('section'), may hold values from -0.125 to 0.125
- neighbours: int32 [9, 1536], P(None, 'patch'), may hold values from 0 to 1535, as said below
Outputs:
- input_grads: bfloat16 [4, 4, 8, 1536, 256], P('section', None, 'dp', 'patch')
- weight_grads: bfloat16 [4, 2304, 256], P('section')
Inputs may be any that keep to these rules, and one draw needn't show every extreme that they name: neighbours[0, p] = p; every entry is (p + d) mod 1536 with -32 <= d <= 32, and both d = 32 and d = -32 occur in every draw.
All inputs are finite; a program needn't handle non-finite values.
Results may differ from a plain program's by a relative error of at most 0.0063.
Values may be sent and summed in bfloat16 or wider, within the bound.
No kernel may reach another device: no remote copies, remote signals or barrier semaphores. Data moves between devices by JAX's collectives and lax.ppermute only.
A program may use at most 64 MiB of HBM per device.

v0:
```python
import functools

import jax
import jax.numpy as jnp
from jax import lax
from jax.experimental import pallas as pl
from jax.experimental.pallas import tpu as pltpu
from jax.sharding import Mesh
from jax.sharding import PartitionSpec as P


HALO = 32
TAPS = 9
C = 256
PIX = 96
LEVELS = 4
REACH = 2 * LEVELS * HALO
TILE = 64
PAD = 32
WIN = PIX + 2 * REACH
ROWS = WIN + 2 * PAD
HALF = TAPS * C // 2
BF = jnp.bfloat16
F32 = jnp.float32
NT = (((1,), (1,)), ((), ()))

FWD_ROWS = ((32, 576), (64, 544), (96, 512), (128, 480))
FWD_TILES = ((0, 9), (1, 9), (1, 8), (2, 8))
PRE_ROWS = ((224, 384), (192, 416), (160, 448), (128, 480))
BWD_ROWS = ((256, 352), (224, 384), (192, 416), (160, 448))
BWD_TILES = ((4, 6), (3, 6), (3, 7), (2, 7))
EDGE = 2 * HALO
OFF = 16
OWN = REACH
HROWS, PROWS, GROWS = PIX, PIX + HALO, PIX
FOLD = PROWS // 2
AT_H, AT_PRE, AT_G = FOLD, FOLD + HROWS, 2 * FOLD + HROWS
MSG = AT_G + GROWS


def expand(gat, t, src, hot):
    rows = jnp.dot(hot, src, preferred_element_type=F32).astype(BF)
    dst = pl.ds(pl.multiple_of(t * TILE, TILE), TILE)
    gat[dst, :C] = src[PAD:PAD + TILE]
    for k in range(1, TAPS):
        gat[dst, k * C:(k + 1) * C] = rows[(k - 1) * TILE:k * TILE]


def expand_all(gat, first, last, src_ref, hot_ref, group):
    def one(t):
        expand(gat, t, src_ref[pl.ds(pl.multiple_of(t * TILE, TILE), 2 * TILE), :], hot_ref[t])

    def some(i, carry):
        for j in range(group):
            one(first + i * group + j)
        return carry

    whole = (last - first) // group
    if whole:
        lax.fori_loop(0, whole, some, 0)
    for t in range(first + whole * group, last):
        one(t)


def pack_kernel(npix, ids_ref, maps, upstream, neighbours, own, to2a, to2b, to3a, to3b, off_buf):
    start, top = maps[0, 0], upstream[0, 0]
    place = ids_ref[2] * PIX + lax.broadcasted_iota(jnp.int32, (TAPS, PIX), 1)
    offsets = neighbours[...] - place + HALO
    offsets = jnp.where(offsets < 0, offsets + npix, offsets)
    offsets = jnp.where(offsets >= npix, offsets - npix, offsets) - HALO
    off_buf[...] = jnp.zeros_like(off_buf)
    off_buf[:TAPS, :PIX] = offsets.astype(F32)
    tail = off_buf[...].astype(BF)
    for ref, rows in ((own, (start, top)), (to2a, (start, top[PIX - HALO:])), (to2b, (start, top[:HALO])),
                      (to3a, (start[PIX - EDGE:],)), (to3b, (start[:EDGE],))):
        at = 0
        for value in (*rows, tail):
            ref[at:at + value.shape[0], :] = value
            at += value.shape[0]


def pack_call(ids, maps, upstream, neighbours):
    npix = PIX * lax.axis_size("py") * lax.axis_size("core")
    mine = pl.BlockSpec((1, 1, PIX, C), lambda i, ids: (ids[1], 0, 0, 0))
    rows = [2 * PIX + OFF, PIX + HALO + OFF, PIX + HALO + OFF, EDGE + OFF, EDGE + OFF]
    return pl.pallas_call(
        functools.partial(pack_kernel, npix),
        grid_spec=pltpu.PrefetchScalarGridSpec(
            num_scalar_prefetch=1,
            grid=(1,),
            in_specs=[mine, mine, pl.BlockSpec((TAPS, PIX), lambda i, ids: (0, 0))],
            out_specs=[pl.BlockSpec((n, C), lambda i, ids: (0, 0)) for n in rows],
            scratch_shapes=[pltpu.VMEM((OFF, C), F32)],
        ),
        out_shape=[jax.ShapeDtypeStruct((n, C), BF) for n in rows],
        interpret=INTERPRET,
        cost_estimate=pl.CostEstimate(flops=0, bytes_accessed=10**6, transcendentals=0),
    )(ids, maps, upstream, neighbours)


def prep_kernel(ids_ref, m3a, m2a, m1a, own, m1b, m2b, m3b, w_own, near_mine, near_other,
                h_ref, g_ref, s_ref, st_ref, gat_ref, pair_ref, w_ref, off_buf, sems):
    core, section = ids_ref[0], ids_ref[1]
    left, right = lax.rem(section + 3, LEVELS), lax.rem(section + 1, LEVELS)
    copies = []
    for n, (src, level) in enumerate((
        (w_own, section),
        (near_mine, jnp.where(core == 0, left, right)),
        (near_other, jnp.where(core == 0, right, left)),
    )):
        copies.append(pltpu.make_async_copy(src, w_ref.at[level], sems.at[n]))
        copies[-1].start()
    h_ref[:PAD, :] = jnp.zeros((PAD, C), BF)
    h_ref[ROWS - PAD:, :] = jnp.zeros((PAD, C), BF)
    g_ref[...] = jnp.zeros_like(g_ref)
    off_buf[:PAD, :] = jnp.zeros((PAD, 128), F32)
    off_buf[ROWS - PAD:, :] = jnp.zeros((PAD, 128), F32)
    at = PAD
    shapes = ((EDGE, PIX - EDGE, 0, 0), (PIX, 0, HALO, PIX - HALO), (PIX, 0, PIX, 0), (PIX, 0, PIX, 0),
              (PIX, 0, PIX, 0), (PIX, 0, HALO, 0), (EDGE, 0, 0, 0))
    for piece, (n, first, n_top, first_top) in zip((m3a, m2a, m1a, own, m1b, m2b, m3b), shapes):
        h_ref[at:at + n, :] = piece[:n, :]
        if n_top:
            place = at + first_top
            g_ref[place:place + n_top, :] = piece[n:n + n_top, :]
        off_t = jnp.transpose(piece[n + n_top:, :128].astype(F32))
        off_buf[at:at + n, :OFF] = off_t[first:first + n]
        at += n

    rel = (lax.broadcasted_iota(jnp.int32, (TILE, 128), 1)
           - lax.broadcasted_iota(jnp.int32, (TILE, 128), 0) - HALO).astype(F32)

    def build_s(t, carry):
        d = off_buf[pl.ds(pl.multiple_of(t * TILE + PAD, PAD), TILE), :]
        for k in range(1, TAPS):
            hit = rel == d[:, k:k + 1]
            s_ref[t, (k - 1) * TILE:k * TILE, :] = jnp.where(hit, 1.0, 0.0).astype(BF)
        return carry

    lax.fori_loop(0, FWD_TILES[0][1], build_s, 0)

    def build_st(t, carry):
        d = jnp.transpose(off_buf[pl.ds(pl.multiple_of(t * TILE, TILE), 128), :])
        for k in range(1, TAPS):
            hit = -rel == d[k:k + 1, :]
            st_ref[t, (k - 1) * TILE:k * TILE, :] = jnp.where(hit, 1.0, 0.0).astype(BF)
        return carry

    lax.fori_loop(BWD_TILES[3][0], BWD_TILES[3][1], build_st, 0)
    expand_all(gat_ref, *FWD_TILES[0], h_ref, s_ref, 3)

    start = pl.multiple_of(PAD + OWN - HALO - PIX * core, HALO)
    offt = jnp.transpose(off_buf[pl.ds(start, 2 * PROWS), :])
    apart = (lax.broadcasted_iota(jnp.int32, (2 * PIX, 2 * PROWS), 0)
             - lax.broadcasted_iota(jnp.int32, (2 * PIX, 2 * PROWS), 1) + HALO).astype(F32)
    for k in range(1, TAPS):
        pair_ref[k - 1] = jnp.where(apart == offt[k:k + 1, :], 1.0, 0.0).astype(BF)
    for copy in copies:
        copy.wait()


def stack_kernel(ids_ref, h0, g_top, s_buf, st_buf, gat0, w_in, far_mine, far_other,
                 out_ref, w_buf, h_buf, gat, der, pre_buf, g_buf, sems):
    core, section = ids_ref[0], ids_ref[1]
    del w_in
    far = w_buf.at[lax.rem(section + 2, LEVELS)]
    copies = []
    for n, (src, dst) in enumerate((
        (far_mine, far.at[pl.ds(pl.multiple_of(core * HALF, HALF), HALF), :]),
        (far_other, far.at[pl.ds(pl.multiple_of((1 - core) * HALF, HALF), HALF), :]),
    )):
        copies.append(pltpu.make_async_copy(src, dst, sems.at[n]))
        copies[-1].start()
    h_buf[...] = jnp.zeros_like(h_buf)
    pre_buf[...] = jnp.zeros_like(pre_buf)
    g_buf[...] = g_top[...]
    for copy in copies:
        copy.wait()

    for level in range(LEVELS):
        first, last = FWD_TILES[level]

        src = h0 if level == 0 else h_buf.at[level - 1]
        rows = gat0 if level == 0 else gat
        if level:
            expand_all(gat, first, last, src, s_buf, 3)
        lo, hi = FWD_ROWS[level]
        act = jnp.dot(rows[lo:hi, :], w_buf[level], preferred_element_type=F32)
        squash = jnp.tanh(act)
        der[level, lo:hi, :] = 1.0 - squash * squash
        if level + 1 < LEVELS:
            h_buf[level, PAD + lo:PAD + hi, :] = (src[PAD + lo:PAD + hi, :].astype(F32) + squash).astype(BF)
        out_ref[level, AT_H:AT_PRE, :] = src[PAD + OWN:PAD + OWN + PIX, :]

    for level in range(LEVELS - 1, -1, -1):
        lo, hi = PRE_ROWS[level]
        pre_buf[PAD + lo:PAD + hi, :] = (
            g_buf[PAD + lo:PAD + hi, :].astype(F32) * der[level, lo:hi, :]).astype(BF)
        first, last = BWD_TILES[level]

        expand_all(gat, first, last, pre_buf, st_buf, 3)
        lo, hi = BWD_ROWS[level]
        total = g_buf[PAD + lo:PAD + hi, :].astype(F32)
        for k in range(TAPS):
            total = total + lax.dot_general(gat[lo:hi, k * C:(k + 1) * C],
                                            w_buf[level, k * C:(k + 1) * C, :], NT,
                                            preferred_element_type=F32)
        g_buf[PAD + lo:PAD + hi, :] = total.astype(BF)
        start = pl.multiple_of(PAD + OWN - HALO + HALO * core, HALO)
        for at, half in ((0, 1 - core), (AT_PRE, core)):
            part = pre_buf[pl.ds(start, PROWS), pl.ds(pl.multiple_of(half * 128, 128), 128)]
            out_ref[level, at:at + FOLD, :128] = part[:FOLD]
            out_ref[level, at:at + FOLD, 128:] = part[FOLD:]
        out_ref[level, AT_G:, :] = g_buf[PAD + OWN:PAD + OWN + PIX, :]


def grad_kernel(core_ref, mine, other, hot, out_ref, gin_ref, p_buf, h_buf, t_buf):
    core = core_ref[0]
    micro = mine.shape[0]
    pair = 2 * PIX
    gin_ref[...] = mine[:, AT_G:, :]
    for c in range(2):
        @pl.when(core == c)
        def _(c=c):
            both = ((mine, AT_PRE), (other, 0))
            for m in range(micro):
                for n, (ref, at) in enumerate(both if c == 0 else both[::-1]):
                    for side in range(2):
                        to = n * PROWS + side * FOLD
                        p_buf[to:to + FOLD, m * 128:(m + 1) * 128] = (
                            ref[m, at:at + FOLD, side * 128:(side + 1) * 128])
                    h_buf[m * pair + n * PIX:m * pair + (n + 1) * PIX, :] = ref[m, AT_H:AT_PRE, :]
    h_t = jnp.transpose(h_buf[...].astype(F32)).astype(BF)
    pre = p_buf[...]
    for k in range(TAPS):
        if k == 0:
            spread = pre[HALO:HALO + pair]
        else:
            spread = jnp.dot(hot[k - 1], pre, preferred_element_type=F32).astype(BF)
        for m in range(micro):
            t_buf[m * pair:(m + 1) * pair, k * 128:(k + 1) * 128] = spread[:, m * 128:(m + 1) * 128]
        if k % 2 or k == TAPS - 1:
            low = k - k % 2 if k < TAPS - 1 else k
            block = jnp.dot(h_t, t_buf[:, low * 128:(k + 1) * 128], preferred_element_type=F32).astype(BF)
            for j in range(low, k + 1):
                out_ref[j * C:(j + 1) * C, :] = block[:, (j - low) * 128:(j - low + 1) * 128]


def sum_kernel(size, x_ref, out_ref):
    pairs = x_ref.shape[0] // (2 * size)
    total = x_ref[:2 * size, :].astype(F32)
    for n in range(1, pairs):
        total = total + x_ref[2 * size * n:2 * size * (n + 1), :].astype(F32)
    total = total[:size] + total[size:]
    total = jnp.concatenate([total, total]).astype(BF)
    for n in range(pairs):
        out_ref[2 * size * n:2 * size * (n + 1), :] = total


def place_kernel(side, core_ref, half, *refs):
    out_ref, sem = refs[-2:]
    column = pl.multiple_of(jnp.abs(core_ref[0] - side) * 128, 128)
    copy = pltpu.make_async_copy(half, out_ref.at[:, pl.ds(column, 128)], sem)
    copy.start()
    copy.wait()


VMEM = pl.BlockSpec(memory_space=pltpu.VMEM)
SMEM = pl.BlockSpec(memory_space=pltpu.SMEM)
ANY = pl.BlockSpec(memory_space=pl.ANY)
INTERPRET = False


def call(kernel, out_shape, in_specs, scratch=(), flops=0, nbytes=0, aliases=None, out_spec=None):
    many = isinstance(out_shape, (tuple, list))
    return pl.pallas_call(
        kernel,
        out_shape=out_shape,
        in_specs=in_specs,
        out_specs=[VMEM] * len(out_shape) if many else out_spec or VMEM,
        scratch_shapes=list(scratch),
        interpret=INTERPRET,
        input_output_aliases=aliases or {},
        cost_estimate=pl.CostEstimate(flops=flops, bytes_accessed=nbytes, transcendentals=0),
        compiler_params=pltpu.CompilerParams(vmem_limit_bytes=28 << 20),
    )


def prep_call(*operands):
    tiles, hot = FWD_TILES[0][1], (TAPS - 1) * TILE
    return call(
        prep_kernel,
        [
            jax.ShapeDtypeStruct((ROWS, C), BF),
            jax.ShapeDtypeStruct((ROWS, C), BF),
            jax.ShapeDtypeStruct((tiles, hot, 2 * TILE), BF),
            jax.ShapeDtypeStruct((BWD_TILES[3][1], hot, 2 * TILE), BF),
            jax.ShapeDtypeStruct((tiles * TILE, TAPS * C), BF),
            jax.ShapeDtypeStruct((TAPS - 1, 2 * PIX, 2 * PROWS), BF),
            jax.ShapeDtypeStruct((LEVELS, TAPS * C, C), BF),
        ],
        [SMEM] + [VMEM] * 7 + [ANY] * 3,
        [pltpu.VMEM((ROWS, 128), F32), pltpu.SemaphoreType.DMA((3,))],
        flops=10**9, nbytes=12 * 10**6,
    )(*operands)


def stack_call(*operands):
    tiles = FWD_TILES[0][1]
    return call(
        stack_kernel,
        [jax.ShapeDtypeStruct((LEVELS, MSG, C), BF), jax.ShapeDtypeStruct((LEVELS, TAPS * C, C), BF)],
        [SMEM] + [VMEM] * 6 + [ANY] * 2,
        [
            pltpu.VMEM((LEVELS - 1, ROWS, C), BF),
            pltpu.VMEM((tiles * TILE, TAPS * C), BF),
            pltpu.VMEM((LEVELS, tiles * TILE, C), F32),
            pltpu.VMEM((ROWS, C), BF),
            pltpu.VMEM((ROWS, C), BF),
            pltpu.SemaphoreType.DMA((2,)),
        ],
        flops=5 * 10**9, nbytes=10 * 10**6, aliases={6: 1},
    )(*operands)


def shift(axis_size, by):
    return [(i, (i + by) % axis_size) for i in range(axis_size)]


def step(maps, upstream, weights, neighbours):
    micro = maps.shape[0]
    section = lax.axis_index("section")
    core = lax.axis_index("core")
    patches = lax.axis_size("py") * lax.axis_size("core")
    patch = lax.axis_index("py") * lax.axis_size("core") + core
    cores = jnp.stack([core, section, patch]).astype(jnp.int32)

    sections = lax.axis_size("section")
    ways = [(2 * i + c, 2 * ((i + (1, -1)[c]) % sections) + c) for i in range(sections) for c in range(2)]
    near = lax.ppermute(weights[0], ("section", "core"), ways)
    half = lax.dynamic_slice_in_dim(near, core * HALF, HALF)
    far = lax.ppermute(half, ("section", "core"), ways)
    near_other = lax.ppermute(near, "core", shift(2, 1))
    far_other = lax.ppermute(far, "core", shift(2, 1))

    own, to2a, to2b, to3a, to3b = pack_call(cores, maps, upstream, neighbours)
    send = functools.partial(lax.ppermute, axis_name=("py", "core"))
    sends = []
    for block, by in ((to2b, -2), (own, -1), (own, 1), (to2a, 2), (to3b, -3), (to3a, 3)):
        sends.append(send(block, perm=shift(patches, by)))
    m2b, m1b, m1a, m2a, m3b, m3a = sends
    h0, g_top, s_hot, st_hot, gat0, hot, w_all = prep_call(
        cores, m3a, m2a, m1a, own, m1b, m2b, m3b, weights[0], near, near_other)
    out, _ = stack_call(cores, h0, g_top, s_hot, st_hot, gat0, w_all, far, far_other)

    mine = lax.all_to_all(out, "section", 0, 0, tiled=True)
    other = lax.ppermute(mine[:, :AT_PRE], "core", shift(2, 1))
    chips = lax.axis_size("dp") * lax.axis_size("py")
    rows = TAPS * C
    blocks = (chips, rows // chips // 4, 4, 128)
    part, gin = call(
        grad_kernel,
        [jax.ShapeDtypeStruct((rows, 128), BF), jax.ShapeDtypeStruct((micro, PIX, C), BF)],
        [SMEM] + [VMEM] * 3,
        [
            pltpu.VMEM((2 * PROWS, micro * 128), BF),
            pltpu.VMEM((micro * 2 * PIX, C), BF),
            pltpu.VMEM((micro * 2 * PIX, TAPS * 128), BF),
        ],
        flops=10**9, nbytes=2 * 10**6,
    )(cores, mine, other, hot)
    pieces = lax.all_to_all(part.reshape(blocks), ("dp", "py"), 0, 0, tiled=True)
    total = call(
        functools.partial(sum_kernel, rows // chips), jax.ShapeDtypeStruct((rows, 128), BF), [VMEM], nbytes=10**6,
    )(pieces.reshape((rows, 128)))
    full = lax.all_to_all(total.reshape(blocks), ("dp", "py"), 0, 0, tiled=True).reshape((rows, 128))
    swapped = lax.ppermute(full, "core", shift(2, 1))
    out_shape = jax.ShapeDtypeStruct((rows, C), BF)
    sem = [pltpu.SemaphoreType.DMA]
    half_done = call(functools.partial(place_kernel, 0), out_shape, [SMEM, ANY], sem, nbytes=10**6, out_spec=ANY)(
        cores, full)
    summed = call(functools.partial(place_kernel, 1), out_shape, [SMEM, ANY, ANY], sem, nbytes=10**6, aliases={2: 0},
                  out_spec=ANY)(cores, swapped, half_done)
    return (gin[None, :, None], summed[None])


def solution(mesh):
    size = dict(mesh.shape)
    grid = (size["dp"], size["section"], size["patch"] // 2, 2)
    fine = Mesh(mesh.devices.reshape(grid), ("dp", "section", "py", "core"))
    patch = ("py", "core")
    in_specs = (
        P(None, "dp", patch, None),
        P(None, "dp", patch, None),
        P("section", None, None),
        P(None, patch),
    )
    out_specs = (P("section", None, "dp", patch, None), P("section", None, None))
    return jax.shard_map(step, mesh=fine, in_specs=in_specs, out_specs=out_specs, check_vma=False)
```

profile of v0, /device:TPU:1, one launch (start us, length us, event | category | flops | bytes accessed | tf_op | source)
XLA Modules:
  0.0 166.5 jit_solution(6133262026671498054)
XLA Ops:
  0.6 5.3 %collective-permute-start.6 = (bf16[2304,256]{1,0:T(8,128)(2,1)}, bf16[2304,256]{1,0:T(8,128)(2,1)S(1)}, u32[]{:S(2)}, u32[]{:S(2)}) collective-permute-start(bf16[2304,256]{1,0:T(8,128)(2,1)} %bitcast.16), channel_id=1, source_target_pairs={{0,16},{1,49},{16,32},{17,1},{32,48},{33,17},{48,0},{49,33},{2,18}... | collective-permute-start | bytes 3538952 | tf_op jit(solution)/shard_map/ppermute | solution.py:340
  6.0 13.4 %collective-permute-done.6.near_mine = bf16[2304,256]{1,0:T(8,128)(2,1)S(1)} collective-permute-done((bf16[2304,256]{1,0:T(8,128)(2,1)}, bf16[2304,256]{1,0:T(8,128)(2,1)S(1)}, u32[]{:S(2)}, u32[]{:S(2)}) %collective-permute-start.6) | collective-permute-done | bytes 1179680 | tf_op jit(solution)/shard_map/ppermute | solution.py:340
  19.4 9.6 %collective-permute-start.7 = (bf16[2304,256]{1,0:T(8,128)(2,1)S(1)}, bf16[2304,256]{1,0:T(8,128)(2,1)S(1)}, u32[]{:S(2)}, u32[]{:S(2)}) collective-permute-start(bf16[2304,256]{1,0:T(8,128)(2,1)S(1)} %collective-permute-done.6.near_mine), channel_id=1, source_target_pairs={{0,1},{1,0},{2,3},{3,2},{4,5},{5,4},{6,7},{7,6},{8,9},{9,8},{10,11... | collective-permute-start | bytes 3538952 | tf_op jit(solution)/shard_map/ppermute | solution.py:343
  29.1 1.9 %collective-permute-start.8 = (bf16[1152,256]{1,0:T(8,128)(2,1)S(1)}, bf16[1152,256]{1,0:T(8,128)(2,1)}, u32[]{:S(2)}, u32[]{:S(2)}) collective-permute-start(bf16[1152,256]{1,0:T(8,128)(2,1)S(1)} %constant_dynamic-slice_fusion), channel_id=1, source_target_pairs={{0,16},{1,49},{16,32},{17,1},{32,48},{33,17},{48,0},{49,33},{2,18}... | collective-permute-start | bytes 1769480 | tf_op jit(solution)/shard_map/ppermute | solution.py:342
  31.0 9.1 %collective-permute-done.8.far_mine = bf16[1152,256]{1,0:T(8,128)(2,1)} collective-permute-done((bf16[1152,256]{1,0:T(8,128)(2,1)S(1)}, bf16[1152,256]{1,0:T(8,128)(2,1)}, u32[]{:S(2)}, u32[]{:S(2)}) %collective-permute-start.8) | collective-permute-done | bytes 589856 | tf_op jit(solution)/shard_map/ppermute | solution.py:342
  40.1 4.0 %collective-permute-start.9 = (bf16[1152,256]{1,0:T(8,128)(2,1)}, bf16[1152,256]{1,0:T(8,128)(2,1)}, u32[]{:S(2)}, u32[]{:S(2)}) collective-permute-start(bf16[1152,256]{1,0:T(8,128)(2,1)} %collective-permute-done.8.far_mine), channel_id=1, source_target_pairs={{0,1},{1,0},{2,3},{3,2},{4,5},{5,4},{6,7},{7,6},{8,9},{9,8},{10,11... | collective-permute-start | bytes 1769480 | tf_op jit(solution)/shard_map/ppermute | solution.py:344
  44.7 2.2 %shard_map.59 = (bf16[208,256]{1,0:T(8,128)(2,1)}, bf16[144,256]{1,0:T(8,128)(2,1)}, bf16[144,256]{1,0:T(8,128)(2,1)}, bf16[80,256]{1,0:T(8,128)(2,1)}, bf16[80,256]{1,0:T(8,128)(2,1)}) custom-call(s32[3]{0:T(128)} %pad_add_fusion.ids_ref.core_ref, bf16[4,1,96,256]{3,2,1,0:T(8,128)(2,1)} %maps.1, bf16[4,1,96,256]{3,2,1,0:T(8,128)(2,1)} %upstream.1, ...), custom_call_target="tpu_custom_call" | custom-call | bytes 1000000 | tf_op jit(solution)/shard_map/pallas_call | solution.py:86
  46.9 1.9 %collective-permute-start = (bf16[80,256]{1,0:T(8,128)(2,1)}, bf16[80,256]{1,0:T(8,128)(2,1)S(1)}, u32[]{:S(2)}, u32[]{:S(2)}) collective-permute-start(bf16[80,256]{1,0:T(8,128)(2,1)} %get-tuple-element.17), channel_id=1, source_target_pairs={{0,3},{1,4},{2,5},{3,6},{4,7},{5,8},{6,9},{7,10},{8,11},{9,12},{10... | collective-permute-start | bytes 122888 | tf_op jit(solution)/shard_map/ppermute | solution.py:350
  48.9 1.9 %collective-permute-start.1 = (bf16[144,256]{1,0:T(8,128)(2,1)}, bf16[144,256]{1,0:T(8,128)(2,1)S(1)}, u32[]{:S(2)}, u32[]{:S(2)}) collective-permute-start(bf16[144,256]{1,0:T(8,128)(2,1)} %get-tuple-element.18), channel_id=1, source_target_pairs={{0,2},{1,3},{2,4},{3,5},{4,6},{5,7},{6,8},{7,9},{8,10},{9,11},{10,... | collective-permute-start | bytes 221192 | tf_op jit(solution)/shard_map/ppermute | solution.py:350
  50.8 4.9 %collective-permute-start.5 = (bf16[80,256]{1,0:T(8,128)(2,1)}, bf16[80,256]{1,0:T(8,128)(2,1)S(1)}, u32[]{:S(2)}, u32[]{:S(2)}) collective-permute-start(bf16[80,256]{1,0:T(8,128)(2,1)} %get-tuple-element.21), channel_id=1, source_target_pairs={{0,13},{1,14},{2,15},{3,0},{4,1},{5,2},{6,3},{7,4},{8,5},{9,6},{10... | collective-permute-start | bytes 122888 | tf_op jit(solution)/shard_map/ppermute | solution.py:350
  57.2 1.6 collective-permute-start.2
  58.8 4.5 %collective-permute-start.4 = (bf16[144,256]{1,0:T(8,128)(2,1)}, bf16[144,256]{1,0:T(8,128)(2,1)S(1)}, u32[]{:S(2)}, u32[]{:S(2)}) collective-permute-start(bf16[144,256]{1,0:T(8,128)(2,1)} %get-tuple-element.20), channel_id=1, source_target_pairs={{0,14},{1,15},{2,0},{3,1},{4,2},{5,3},{6,4},{7,5},{8,6},{9,7},{10,... | collective-permute-start | bytes 221192 | tf_op jit(solution)/shard_map/ppermute | solution.py:350
  63.3 1.7 %collective-permute-done.4.m2b = bf16[144,256]{1,0:T(8,128)(2,1)S(1)} collective-permute-done((bf16[144,256]{1,0:T(8,128)(2,1)}, bf16[144,256]{1,0:T(8,128)(2,1)S(1)}, u32[]{:S(2)}, u32[]{:S(2)}) %collective-permute-start.4) | collective-permute-done | bytes 73760 | tf_op jit(solution)/shard_map/ppermute | solution.py:350
  66.6 4.6 %shard_map.60 = (bf16[672,256]{1,0:T(8,128)(2,1)S(1)}, bf16[672,256]{1,0:T(8,128)(2,1)S(1)}, bf16[9,512,128]{2,1,0:T(8,128)(2,1)S(1)}, bf16[7,512,128]{2,1,0:T(8...) custom-call(s32[3]{0:T(128)S(1)} %copy-done.2, ...), custom_call_target="tpu_custom_call" | custom-call | flops 1000000000 | bytes 12000000 | tf_op jit(solution)/shard_map/pallas_call | solution.py:291
  71.1 12.0 %shard_map.61 = (bf16[4,320,256]{2,1,0:T(8,128)(2,1)S(1)}, bf16[4,2304,256]{2,1,0:T(8,128)(2,1)S(1)}) custom-call(s32[3]{0:T(128)S(1)} %copy-done.2, bf16[672,256]{1,0:T(8,128)(2,1)S(1)} %get-tuple-element.22.h0, bf16[672,256]{1,0:T(8,128)(2,1)S(1)} %get-tuple-element.23.g_top, ...), custom_call_target="tpu_custom_call", output_to_operand_aliasing={{1}: (6, {})} | custom-call | flops 5000000000 | bytes 10000000 | tf_op jit(solution)/shard_map/pallas_call | solution.py:310
  83.1 12.2 %all_to_all.15.mine = bf16[4,320,256]{2,1,0:T(8,128)(2,1)S(1)} all-to-all(bf16[4,320,256]{2,1,0:T(8,128)(2,1)S(1)} %get-tuple-element.28), channel_id=1, replica_groups=mesh['dp'=8,'section'=4,'py'=8,'core'=2] {'section'}, dimensions={0} | all-to-all | bytes 1310720 | tf_op jit(solution)/shard_map/all_to_all | solution.py:356
  95.4 3.9 %collective-permute-start.10 = (bf16[4,160,256]{2,1,0:T(8,128)(2,1)S(1)}, bf16[4,160,256]{2,1,0:T(8,128)(2,1)S(1)}, u32[]{:S(2)}, u32[]{:S(2)}) collective-permute-start(bf16[4,160,256]{2,1,0:T(8,128)(2,1)S(1)} %slice.4), channel_id=1, source_target_pairs={{0,1},{1,0},{2,3},{3,2},{4,5},{5,4},{6,7},{7,6},{8,9},{9,8},{10,11... | collective-permute-start | bytes 983048 | tf_op jit(solution)/shard_map/ppermute | solution.py:357
  99.3 1.2 collective-permute-done.10.other
  100.5 1.9 %shard_map.62 = (bf16[2304,128]{1,0:T(8,128)(2,1)S(1)}, bf16[4,96,256]{2,1,0:T(8,128)(2,1)}) custom-call(s32[3]{0:T(128)S(1)} %copy-done.2, bf16[4,320,256]{2,1,0:T(8,128)(2,1)S(1)} %all_to_all.15.mine, bf16[4,160,256]{2,1,0:T(8,128)(2,1)S(1)} %collective-permute-done.10.other, bf16[8,192,256]{2,1,0:T(8,128)(2,1)S(1)} %get-tuple-element.29.hot), custom_call_target="tpu_custom_call" | custom-call | flops 1000000000 | bytes 2000000 | tf_op jit(solution)/shard_map/pallas_call | solution.py:361
  102.4 30.6 %all_to_all.16 = bf16[64,9,4,128]{3,2,1,0:T(4,128)(2,1)S(1)} all-to-all(bf16[64,9,4,128]{3,2,1,0:T(4,128)(2,1)S(1)} %bitcast.18), channel_id=1, replica_groups=mesh['dp'=8,'section'=4,'py'=8,'core'=2] {'dp','py'}, dimensions={0} | all-to-all | bytes 1179648 | tf_op jit(solution)/shard_map/all_to_all | solution.py:372
  133.1 24.4 %all_to_all.17 = bf16[64,9,4,128]{3,2,1,0:T(4,128)(2,1)S(1)} all-to-all(bf16[64,9,4,128]{3,2,1,0:T(4,128)(2,1)S(1)} %bitcast.13), channel_id=1, replica_groups=mesh['dp'=8,'section'=4,'py'=8,'core'=2] {'dp','py'}, dimensions={0} | all-to-all | bytes 1179648 | tf_op jit(solution)/shard_map/all_to_all | solution.py:376
  157.5 6.0 %collective-permute-start.11 = (bf16[2304,128]{1,0:T(8,128)(2,1)S(1)}, bf16[2304,128]{1,0:T(8,128)(2,1)S(1)}, u32[]{:S(2)}, u32[]{:S(2)}) collective-permute-start(bf16[2304,128]{1,0:T(8,128)(2,1)S(1)} %bitcast.14), channel_id=1, source_target_pairs={{0,1},{1,0},{2,3},{3,2},{4,5},{5,4},{6,7},{7,6},{8,9},{9,8},{10,11... | collective-permute-start | bytes 1769480 | tf_op jit(solution)/shard_map/ppermute | solution.py:377
  163.5 1.4 shard_map.64.refs_0_
  165.2 1.4 shard_map.65
  (19 shorter events, 4.1 us)
Async XLA Ops:
  0.6 64.4 %copy-start = (bf16[1,2304,256]{2,1,0:T(8,128)(2,1)S(1)}, bf16[1,2304,256]{2,1,0:T(8,128)(2,1)}, u32[]{:S(2)}) copy-start(bf16[1,2304,256]{2,1,0:T(8,128)(2,1)} %param.6) | copy-start | bytes 3538948
  0.6 18.8 %collective-permute-start.6 = (bf16[2304,256]{1,0:T(8,128)(2,1)}, bf16[2304,256]{1,0:T(8,128)(2,1)S(1)}, u32[]{:S(2)}, u32[]{:S(2)}) collective-permute-start(bf16[2304,256]{1,0:T(8,128)(2,1)} %bitcast.16), channel_id=1, source_target_pairs={{0,16},{1,49},{16,32},{17,1},{32,48},{33,17},{48,0},{49,33},{2,18}... | collective-permute-start | bytes 3538952 | tf_op jit(solution)/shard_map/ppermute | solution.py:340
  19.4 45.6 %collective-permute-start.7 = (bf16[2304,256]{1,0:T(8,128)(2,1)S(1)}, bf16[2304,256]{1,0:T(8,128)(2,1)S(1)}, u32[]{:S(2)}, u32[]{:S(2)}) collective-permute-start(bf16[2304,256]{1,0:T(8,128)(2,1)S(1)} %collective-permute-done.6.near_mine), channel_id=1, source_target_pairs={{0,1},{1,0},{2,3},{3,2},{4,5},{5,4},{6,7},{7,6},{8,9},{9,8},{10,11... | collective-permute-start | bytes 3538952 | tf_op jit(solution)/shard_map/ppermute | solution.py:343
  29.1 11.0 %collective-permute-start.8 = (bf16[1152,256]{1,0:T(8,128)(2,1)S(1)}, bf16[1152,256]{1,0:T(8,128)(2,1)}, u32[]{:S(2)}, u32[]{:S(2)}) collective-permute-start(bf16[1152,256]{1,0:T(8,128)(2,1)S(1)} %constant_dynamic-slice_fusion), channel_id=1, source_target_pairs={{0,16},{1,49},{16,32},{17,1},{32,48},{33,17},{48,0},{49,33},{2,18}... | collective-permute-start | bytes 1769480 | tf_op jit(solution)/shard_map/ppermute | solution.py:342
  40.1 31.0 %collective-permute-start.9 = (bf16[1152,256]{1,0:T(8,128)(2,1)}, bf16[1152,256]{1,0:T(8,128)(2,1)}, u32[]{:S(2)}, u32[]{:S(2)}) collective-permute-start(bf16[1152,256]{1,0:T(8,128)(2,1)} %collective-permute-done.8.far_mine), channel_id=1, source_target_pairs={{0,1},{1,0},{2,3},{3,2},{4,5},{5,4},{6,7},{7,6},{8,9},{9,8},{10,11... | collective-permute-start | bytes 1769480 | tf_op jit(solution)/shard_map/ppermute | solution.py:344
  46.9 8.7 %collective-permute-start = (bf16[80,256]{1,0:T(8,128)(2,1)}, bf16[80,256]{1,0:T(8,128)(2,1)S(1)}, u32[]{:S(2)}, u32[]{:S(2)}) collective-permute-start(bf16[80,256]{1,0:T(8,128)(2,1)} %get-tuple-element.17), channel_id=1, source_target_pairs={{0,3},{1,4},{2,5},{3,6},{4,7},{5,8},{6,9},{7,10},{8,11},{9,12},{10... | collective-permute-start | bytes 122888 | tf_op jit(solution)/shard_map/ppermute | solution.py:350
  48.9 9.9 %collective-permute-start.1 = (bf16[144,256]{1,0:T(8,128)(2,1)}, bf16[144,256]{1,0:T(8,128)(2,1)S(1)}, u32[]{:S(2)}, u32[]{:S(2)}) collective-permute-start(bf16[144,256]{1,0:T(8,128)(2,1)} %get-tuple-element.18), channel_id=1, source_target_pairs={{0,2},{1,3},{2,4},{3,5},{4,6},{5,7},{6,8},{7,9},{8,10},{9,11},{10,... | collective-permute-start | bytes 221192 | tf_op jit(solution)/shard_map/ppermute | solution.py:350
  50.8 6.4 %collective-permute-start.5 = (bf16[80,256]{1,0:T(8,128)(2,1)}, bf16[80,256]{1,0:T(8,128)(2,1)S(1)}, u32[]{:S(2)}, u32[]{:S(2)}) collective-permute-start(bf16[80,256]{1,0:T(8,128)(2,1)} %get-tuple-element.21), channel_id=1, source_target_pairs={{0,13},{1,14},{2,15},{3,0},{4,1},{5,2},{6,3},{7,4},{8,5},{9,6},{10... | collective-permute-start | bytes 122888 | tf_op jit(solution)/shard_map/ppermute | solution.py:350
  55.6 9.4 %collective-permute-start.3 = (bf16[208,256]{1,0:T(8,128)(2,1)}, bf16[208,256]{1,0:T(8,128)(2,1)S(1)}, u32[]{:S(2)}, u32[]{:S(2)}) collective-permute-start(bf16[208,256]{1,0:T(8,128)(2,1)} %get-tuple-element.19.own), channel_id=1, source_target_pairs={{0,15},{1,0},{2,1},{3,2},{4,3},{5,4},{6,5},{7,6},{8,7},{9,8},{10,9... | collective-permute-start | bytes 319496 | tf_op jit(solution)/shard_map/ppermute | solution.py:350
  57.2 7.8 %collective-permute-start.2 = (bf16[208,256]{1,0:T(8,128)(2,1)}, bf16[208,256]{1,0:T(8,128)(2,1)S(1)}, u32[]{:S(2)}, u32[]{:S(2)}) collective-permute-start(bf16[208,256]{1,0:T(8,128)(2,1)} %get-tuple-element.19.own), channel_id=1, source_target_pairs={{0,1},{1,2},{2,3},{3,4},{4,5},{5,6},{6,7},{7,8},{8,9},{9,10},{10,1... | collective-permute-start | bytes 319496 | tf_op jit(solution)/shard_map/ppermute | solution.py:350
  58.8 6.2 %collective-permute-start.4 = (bf16[144,256]{1,0:T(8,128)(2,1)}, bf16[144,256]{1,0:T(8,128)(2,1)S(1)}, u32[]{:S(2)}, u32[]{:S(2)}) collective-permute-start(bf16[144,256]{1,0:T(8,128)(2,1)} %get-tuple-element.20), channel_id=1, source_target_pairs={{0,14},{1,15},{2,0},{3,1},{4,2},{5,3},{6,4},{7,5},{8,6},{9,7},{10,... | collective-permute-start | bytes 221192 | tf_op jit(solution)/shard_map/ppermute | solution.py:350
  65.0 0.9 copy-start.1
  65.9 0.6 copy-start.2
  95.4 5.2 %collective-permute-start.10 = (bf16[4,160,256]{2,1,0:T(8,128)(2,1)S(1)}, bf16[4,160,256]{2,1,0:T(8,128)(2,1)S(1)}, u32[]{:S(2)}, u32[]{:S(2)}) collective-permute-start(bf16[4,160,256]{2,1,0:T(8,128)(2,1)S(1)} %slice.4), channel_id=1, source_target_pairs={{0,1},{1,0},{2,3},{3,2},{4,5},{5,4},{6,7},{7,6},{8,9},{9,8},{10,11... | collective-permute-start | bytes 983048 | tf_op jit(solution)/shard_map/ppermute | solution.py:357
  157.5 7.7 %collective-permute-start.11 = (bf16[2304,128]{1,0:T(8,128)(2,1)S(1)}, bf16[2304,128]{1,0:T(8,128)(2,1)S(1)}, u32[]{:S(2)}, u32[]{:S(2)}) collective-permute-start(bf16[2304,128]{1,0:T(8,128)(2,1)S(1)} %bitcast.14), channel_id=1, source_target_pairs={{0,1},{1,0},{2,3},{3,2},{4,5},{5,4},{6,7},{7,6},{8,9},{9,8},{10,11... | collective-permute-start | bytes 1769480 | tf_op jit(solution)/shard_map/ppermute | solution.py:377
where the time goes:
time: 167 us
  blocking collectives  67.2 us (40%)
  starting transfers between devices  46.5 us (28%)
  waiting for transfers between devices  26.4 us (16%)
  Pallas kernels  23.5 us (14%)
    all_to_all x1, blocking collectives, step(): lax.all_to_all(part.reshape(blocks), ('dp', 'py'), 0, 0, tiled=True)  30.6 us
    all_to_all x1, blocking collectives, step(): lax.all_to_all(total.reshape(blocks), ('dp', 'py'), 0, 0, tiled=True)  24.4 us
    ppermute x6, starting transfers between devices, step(): sends.append(send(block, perm=shift(patches, by)))  15.7 us
    ppermute x1, waiting for transfers between devices, step(): near = lax.ppermute(weights[0], ('section', 'core'), ways)  13.4 us
    all_to_all x1, blocking collectives, step(): mine = lax.all_to_all(out, 'section', 0, 0, tiled=True)  12.2 us
    pallas_call x1, Pallas kernels, stack_call(): call(stack_kernel, [jax.ShapeDtypeStruct((LEVELS, MSG, C), BF), jax.Shape...  12 us
    ppermute x1, starting transfers between devices, step(): near_other = lax.ppermute(near, 'core', shift(2, 1))  9.6 us
    ppermute x1, waiting for transfers between devices, step(): far = lax.ppermute(half, ('section', 'core'), ways)  9.1 us
  transfers between devices with their start and end apart: 12, of which 6 were waited for; matrix products, arithmetic and copies ran while one was open for 0% of the time, Pallas kernels for 5%

commit v1 on v0

--- a/solution.py
+++ b/solution.py
@@ -98,7 +98,7 @@
     )(ids, maps, upstream, neighbours)
 
 
-def prep_kernel(ids_ref, m3a, m2a, m1a, own, m1b, m2b, m3b, w_own, near_mine, near_other,
+def prep_kernel(ids_ref, m3a, m2a, m1a, own, m1b, m2b, m3b, w_own, near_mine,
                 h_ref, g_ref, s_ref, st_ref, gat_ref, pair_ref, w_ref, off_buf, sems):
     core, section = ids_ref[0], ids_ref[1]
     left, right = lax.rem(section + 3, LEVELS), lax.rem(section + 1, LEVELS)
@@ -106,7 +106,6 @@
     for n, (src, level) in enumerate((
         (w_own, section),
         (near_mine, jnp.where(core == 0, left, right)),
-        (near_other, jnp.where(core == 0, right, left)),
     )):
         copies.append(pltpu.make_async_copy(src, w_ref.at[level], sems.at[n]))
         copies[-1].start()
@@ -159,13 +158,14 @@
         copy.wait()
 
 
-def stack_kernel(ids_ref, h0, g_top, s_buf, st_buf, gat0, w_in, far_mine, far_other,
+def stack_kernel(ids_ref, h0, g_top, s_buf, st_buf, gat0, w_in, near_other, far_mine, far_other,
                  out_ref, w_buf, h_buf, gat, der, pre_buf, g_buf, sems):
     core, section = ids_ref[0], ids_ref[1]
     del w_in
     far = w_buf.at[lax.rem(section + 2, LEVELS)]
     copies = []
     for n, (src, dst) in enumerate((
+        (near_other, w_buf.at[lax.rem(section + 1 + 2 * core, LEVELS)]),
         (far_mine, far.at[pl.ds(pl.multiple_of(core * HALF, HALF), HALF), :]),
         (far_other, far.at[pl.ds(pl.multiple_of((1 - core) * HALF, HALF), HALF), :]),
     )):
@@ -299,8 +299,8 @@
             jax.ShapeDtypeStruct((TAPS - 1, 2 * PIX, 2 * PROWS), BF),
             jax.ShapeDtypeStruct((LEVELS, TAPS * C, C), BF),
         ],
-        [SMEM] + [VMEM] * 7 + [ANY] * 3,
-        [pltpu.VMEM((ROWS, 128), F32), pltpu.SemaphoreType.DMA((3,))],
+        [SMEM] + [VMEM] * 7 + [ANY] * 2,
+        [pltpu.VMEM((ROWS, 128), F32), pltpu.SemaphoreType.DMA((2,))],
         flops=10**9, nbytes=12 * 10**6,
     )(*operands)
 
@@ -310,14 +310,14 @@
     return call(
         stack_kernel,
         [jax.ShapeDtypeStruct((LEVELS, MSG, C), BF), jax.ShapeDtypeStruct((LEVELS, TAPS * C, C), BF)],
-        [SMEM] + [VMEM] * 6 + [ANY] * 2,
+        [SMEM] + [VMEM] * 6 + [ANY] * 3,
         [
             pltpu.VMEM((LEVELS - 1, ROWS, C), BF),
             pltpu.VMEM((tiles * TILE, TAPS * C), BF),
             pltpu.VMEM((LEVELS, tiles * TILE, C), F32),
             pltpu.VMEM((ROWS, C), BF),
             pltpu.VMEM((ROWS, C), BF),
-            pltpu.SemaphoreType.DMA((2,)),
+            pltpu.SemaphoreType.DMA((3,)),
         ],
         flops=5 * 10**9, nbytes=10 * 10**6, aliases={6: 1},
     )(*operands)
@@ -350,8 +350,8 @@
         sends.append(send(block, perm=shift(patches, by)))
     m2b, m1b, m1a, m2a, m3b, m3a = sends
     h0, g_top, s_hot, st_hot, gat0, hot, w_all = prep_call(
-        cores, m3a, m2a, m1a, own, m1b, m2b, m3b, weights[0], near, near_other)
-    out, _ = stack_call(cores, h0, g_top, s_hot, st_hot, gat0, w_all, far, far_other)
+        cores, m3a, m2a, m1a, own, m1b, m2b, m3b, weights[0], near)
+    out, _ = stack_call(cores, h0, g_top, s_hot, st_hot, gat0, w_all, near_other, far, far_other)
 
     mine = lax.all_to_all(out, "section", 0, 0, tiled=True)
     other = lax.ppermute(mine[:, :AT_PRE], "core", shift(2, 1))

time: 167 us -> 165 us (0.988)
  waiting for transfers between devices: 26.4 us -> 17.4 us
  starting transfers between devices: 46.5 us -> 53.5 us
    ppermute x1, waiting for transfers between devices: 9.1 us -> 0.19 us  [step(): far = lax.ppermute(half, ('section', 'core'), ways)]
    ppermute x1, starting transfers between devices: 3.98 us -> 11 us  [step(): far_other = lax.ppermute(far, 'core', shift(2, 1))]
    ppermute x1, starting transfers between devices: 1.92 us -> 4.92 us  [step(): far = lax.ppermute(half, ('section', 'core'), ways)]
    ppermute x1, starting transfers between devices: 9.6 us -> 6.61 us  [step(): near_other = lax.ppermute(near, 'core', shift(2, 1))]
where the time goes in v1:
time: 165 us
  blocking collectives  67.2 us (41%)
  starting transfers between devices  53.5 us (32%)
  Pallas kernels  23.5 us (14%)
  waiting for transfers between devices  17.4 us (11%)
    all_to_all x1, blocking collectives, step(): lax.all_to_all(part.reshape(blocks), ('dp', 'py'), 0, 0, tiled=True)  30.6 us
    all_to_all x1, blocking collectives, step(): lax.all_to_all(total.reshape(blocks), ('dp', 'py'), 0, 0, tiled=True)  24.4 us
    ppermute x6, starting transfers between devices, step(): sends.append(send(block, perm=shift(patches, by)))  15.7 us
    ppermute x1, waiting for transfers between devices, step(): near = lax.ppermute(weights[0], ('section', 'core'), ways)  13.4 us
    pallas_call x1, Pallas kernels, stack_call(): call(stack_kernel, [jax.ShapeDtypeStruct((LEVELS, MSG, C), BF), jax.Shape...  12.2 us
    all_to_all x1, blocking collectives, step(): mine = lax.all_to_all(out, 'section', 0, 0, tiled=True)  12.2 us
    ppermute x1, starting transfers between devices, step(): far_other = lax.ppermute(far, 'core', shift(2, 1))  11 us
    ppermute x1, starting transfers between devices, step(): near_other = lax.ppermute(near, 'core', shift(2, 1))  6.61 us
  transfers between devices with their start and end apart: 12, of which 6 were waited for; matrix products, arithmetic and copies ran while one was open for 0% of the time, Pallas kernels for 5%

profile of v1, /device:TPU:1, one launch (start us, length us, event | category | flops | bytes accessed | tf_op | source)
XLA Modules:
  0.0 164.7 jit_solution(6286880459931674935)
XLA Ops:
  0.6 5.3 %collective-permute-start.6 = (bf16[2304,256]{1,0:T(8,128)(2,1)}, bf16[2304,256]{1,0:T(8,128)(2,1)S(1)}, u32[]{:S(2)}, u32[]{:S(2)}) collective-permute-start(bf16[2304,256]{1,0:T(8,128)(2,1)} %bitcast.17), channel_id=1, source_target_pairs={{0,16},{1,49},{16,32},{17,1},{32,48},{33,17},{48,0},{49,33},{2,18}... | collective-permute-start | bytes 3538952 | tf_op jit(solution)/shard_map/ppermute | solution.py:340
  6.0 13.4 %collective-permute-done.6.near_mine = bf16[2304,256]{1,0:T(8,128)(2,1)S(1)} collective-permute-done((bf16[2304,256]{1,0:T(8,128)(2,1)}, bf16[2304,256]{1,0:T(8,128)(2,1)S(1)}, u32[]{:S(2)}, u32[]{:S(2)}) %collective-permute-start.6) | collective-permute-done | bytes 1179680 | tf_op jit(solution)/shard_map/ppermute | solution.py:340
  19.5 4.9 %collective-permute-start.8 = (bf16[1152,256]{1,0:T(8,128)(2,1)S(1)}, bf16[1152,256]{1,0:T(8,128)(2,1)}, u32[]{:S(2)}, u32[]{:S(2)}) collective-permute-start(bf16[1152,256]{1,0:T(8,128)(2,1)S(1)} %constant_dynamic-slice_fusion), channel_id=1, source_target_pairs={{0,16},{1,49},{16,32},{17,1},{32,48},{33,17},{48,0},{49,33},{2,18}... | collective-permute-start | bytes 1769480 | tf_op jit(solution)/shard_map/ppermute | solution.py:342
  24.4 6.6 %collective-permute-start.7 = (bf16[2304,256]{1,0:T(8,128)(2,1)S(1)}, bf16[2304,256]{1,0:T(8,128)(2,1)S(1)}, u32[]{:S(2)}, u32[]{:S(2)}) collective-permute-start(bf16[2304,256]{1,0:T(8,128)(2,1)S(1)} %collective-permute-done.6.near_mine), channel_id=1, source_target_pairs={{0,1},{1,0},{2,3},{3,2},{4,5},{5,4},{6,7},{7,6},{8,9},{9,8},{10,11... | collective-permute-start | bytes 3538952 | tf_op jit(solution)/shard_map/ppermute | solution.py:343
  31.2 11.0 %collective-permute-start.9 = (bf16[1152,256]{1,0:T(8,128)(2,1)}, bf16[1152,256]{1,0:T(8,128)(2,1)}, u32[]{:S(2)}, u32[]{:S(2)}) collective-permute-start(bf16[1152,256]{1,0:T(8,128)(2,1)} %collective-permute-done.8.far_mine), channel_id=1, source_target_pairs={{0,1},{1,0},{2,3},{3,2},{4,5},{5,4},{6,7},{7,6},{8,9},{9,8},{10,11... | collective-permute-start | bytes 1769480 | tf_op jit(solution)/shard_map/ppermute | solution.py:344
  42.8 2.2 %shard_map.59 = (bf16[208,256]{1,0:T(8,128)(2,1)}, bf16[144,256]{1,0:T(8,128)(2,1)}, bf16[144,256]{1,0:T(8,128)(2,1)}, bf16[80,256]{1,0:T(8,128)(2,1)}, bf16[80,256]{1,0:T(8,128)(2,1)}) custom-call(s32[3]{0:T(128)} %pad_add_fusion.ids_ref.core_ref, bf16[4,1,96,256]{3,2,1,0:T(8,128)(2,1)} %maps.1, bf16[4,1,96,256]{3,2,1,0:T(8,128)(2,1)} %upstream.1, ...), custom_call_target="tpu_custom_call" | custom-call | bytes 1000000 | tf_op jit(solution)/shard_map/pallas_call | solution.py:86
  45.1 1.9 %collective-permute-start = (bf16[80,256]{1,0:T(8,128)(2,1)}, bf16[80,256]{1,0:T(8,128)(2,1)S(1)}, u32[]{:S(2)}, u32[]{:S(2)}) collective-permute-start(bf16[80,256]{1,0:T(8,128)(2,1)} %get-tuple-element.17), channel_id=1, source_target_pairs={{0,3},{1,4},{2,5},{3,6},{4,7},{5,8},{6,9},{7,10},{8,11},{9,12},{10... | collective-permute-start | bytes 122888 | tf_op jit(solution)/shard_map/ppermute | solution.py:350
  47.0 1.9 %collective-permute-start.1 = (bf16[144,256]{1,0:T(8,128)(2,1)}, bf16[144,256]{1,0:T(8,128)(2,1)S(1)}, u32[]{:S(2)}, u32[]{:S(2)}) collective-permute-start(bf16[144,256]{1,0:T(8,128)(2,1)} %get-tuple-element.18), channel_id=1, source_target_pairs={{0,2},{1,3},{2,4},{3,5},{4,6},{5,7},{6,8},{7,9},{8,10},{9,11},{10,... | collective-permute-start | bytes 221192 | tf_op jit(solution)/shard_map/ppermute | solution.py:350
  48.9 4.9 %collective-permute-start.5 = (bf16[80,256]{1,0:T(8,128)(2,1)}, bf16[80,256]{1,0:T(8,128)(2,1)S(1)}, u32[]{:S(2)}, u32[]{:S(2)}) collective-permute-start(bf16[80,256]{1,0:T(8,128)(2,1)} %get-tuple-element.21), channel_id=1, source_target_pairs={{0,13},{1,14},{2,15},{3,0},{4,1},{5,2},{6,3},{7,4},{8,5},{9,6},{10... | collective-permute-start | bytes 122888 | tf_op jit(solution)/shard_map/ppermute | solution.py:350
  53.8 0.9 collective-permute-start.3
  55.3 1.6 collective-permute-start.2
  56.9 4.5 %collective-permute-start.4 = (bf16[144,256]{1,0:T(8,128)(2,1)}, bf16[144,256]{1,0:T(8,128)(2,1)S(1)}, u32[]{:S(2)}, u32[]{:S(2)}) collective-permute-start(bf16[144,256]{1,0:T(8,128)(2,1)} %get-tuple-element.20), channel_id=1, source_target_pairs={{0,14},{1,15},{2,0},{3,1},{4,2},{5,3},{6,4},{7,5},{8,6},{9,7},{10,... | collective-permute-start | bytes 221192 | tf_op jit(solution)/shard_map/ppermute | solution.py:350
  61.4 1.7 %collective-permute-done.4.m2b = bf16[144,256]{1,0:T(8,128)(2,1)S(1)} collective-permute-done((bf16[144,256]{1,0:T(8,128)(2,1)}, bf16[144,256]{1,0:T(8,128)(2,1)S(1)}, u32[]{:S(2)}, u32[]{:S(2)}) %collective-permute-start.4) | collective-permute-done | bytes 73760 | tf_op jit(solution)/shard_map/ppermute | solution.py:350
  64.7 4.3 %shard_map.60 = (bf16[672,256]{1,0:T(8,128)(2,1)S(1)}, bf16[672,256]{1,0:T(8,128)(2,1)S(1)}, bf16[9,512,128]{2,1,0:T(8,128)(2,1)S(1)}, bf16[7,512,128]{2,1,0:T(8...) custom-call(s32[3]{0:T(128)S(1)} %copy-done, ...), custom_call_target="tpu_custom_call" | custom-call | flops 1000000000 | bytes 12000000 | tf_op jit(solution)/shard_map/pallas_call | solution.py:291
  69.0 12.2 %shard_map.61 = (bf16[4,320,256]{2,1,0:T(8,128)(2,1)S(1)}, bf16[4,2304,256]{2,1,0:T(8,128)(2,1)S(1)}) custom-call(s32[3]{0:T(128)S(1)} %copy-done, bf16[672,256]{1,0:T(8,128)(2,1)S(1)} %get-tuple-element.22.h0, bf16[672,256]{1,0:T(8,128)(2,1)S(1)} %get-tuple-element.23.g_top, ...), custom_call_target="tpu_custom_call", output_to_operand_aliasing={{1}: (6, {})} | custom-call | flops 5000000000 | bytes 10000000 | tf_op jit(solution)/shard_map/pallas_call | solution.py:310
  81.3 12.2 %all_to_all.15.mine = bf16[4,320,256]{2,1,0:T(8,128)(2,1)S(1)} all-to-all(bf16[4,320,256]{2,1,0:T(8,128)(2,1)S(1)} %get-tuple-element.28), channel_id=1, replica_groups=mesh['dp'=8,'section'=4,'py'=8,'core'=2] {'section'}, dimensions={0} | all-to-all | bytes 1310720 | tf_op jit(solution)/shard_map/all_to_all | solution.py:356
  93.5 3.9 %collective-permute-start.10 = (bf16[4,160,256]{2,1,0:T(8,128)(2,1)S(1)}, bf16[4,160,256]{2,1,0:T(8,128)(2,1)S(1)}, u32[]{:S(2)}, u32[]{:S(2)}) collective-permute-start(bf16[4,160,256]{2,1,0:T(8,128)(2,1)S(1)} %slice.4), channel_id=1, source_target_pairs={{0,1},{1,0},{2,3},{3,2},{4,5},{5,4},{6,7},{7,6},{8,9},{9,8},{10,11... | collective-permute-start | bytes 983048 | tf_op jit(solution)/shard_map/ppermute | solution.py:357
  97.4 1.2 collective-permute-done.10.other
  98.7 1.9 %shard_map.62 = (bf16[2304,128]{1,0:T(8,128)(2,1)S(1)}, bf16[4,96,256]{2,1,0:T(8,128)(2,1)}) custom-call(s32[3]{0:T(128)S(1)} %copy-done, bf16[4,320,256]{2,1,0:T(8,128)(2,1)S(1)} %all_to_all.15.mine, bf16[4,160,256]{2,1,0:T(8,128)(2,1)S(1)} %collective-permute-done.10.other, bf16[8,192,256]{2,1,0:T(8,128)(2,1)S(1)} %get-tuple-element.29.hot), custom_call_target="tpu_custom_call" | custom-call | flops 1000000000 | bytes 2000000 | tf_op jit(solution)/shard_map/pallas_call | solution.py:361
  100.6 30.6 %all_to_all.16 = bf16[64,9,4,128]{3,2,1,0:T(4,128)(2,1)S(1)} all-to-all(bf16[64,9,4,128]{3,2,1,0:T(4,128)(2,1)S(1)} %bitcast.16), channel_id=1, replica_groups=mesh['dp'=8,'section'=4,'py'=8,'core'=2] {'dp','py'}, dimensions={0} | all-to-all | bytes 1179648 | tf_op jit(solution)/shard_map/all_to_all | solution.py:372
  131.2 24.4 %all_to_all.17 = bf16[64,9,4,128]{3,2,1,0:T(4,128)(2,1)S(1)} all-to-all(bf16[64,9,4,128]{3,2,1,0:T(4,128)(2,1)S(1)} %bitcast.13), channel_id=1, replica_groups=mesh['dp'=8,'section'=4,'py'=8,'core'=2] {'dp','py'}, dimensions={0} | all-to-all | bytes 1179648 | tf_op jit(solution)/shard_map/all_to_all | solution.py:376
  155.6 6.0 %collective-permute-start.11 = (bf16[2304,128]{1,0:T(8,128)(2,1)S(1)}, bf16[2304,128]{1,0:T(8,128)(2,1)S(1)}, u32[]{:S(2)}, u32[]{:S(2)}) collective-permute-start(bf16[2304,128]{1,0:T(8,128)(2,1)S(1)} %bitcast.14), channel_id=1, source_target_pairs={{0,1},{1,0},{2,3},{3,2},{4,5},{5,4},{6,7},{7,6},{8,9},{9,8},{10,11... | collective-permute-start | bytes 1769480 | tf_op jit(solution)/shard_map/ppermute | solution.py:377
  161.7 1.4 shard_map.64.refs_0_
  163.3 1.4 shard_map.65
  (21 shorter events, 3.5 us)
Async XLA Ops:
  0.6 62.5 %copy-start.2 = (bf16[1,2304,256]{2,1,0:T(8,128)(2,1)S(1)}, bf16[1,2304,256]{2,1,0:T(8,128)(2,1)}, u32[]{:S(2)}) copy-start(bf16[1,2304,256]{2,1,0:T(8,128)(2,1)} %param.6) | copy-start | bytes 3538948
  0.6 18.8 %collective-permute-start.6 = (bf16[2304,256]{1,0:T(8,128)(2,1)}, bf16[2304,256]{1,0:T(8,128)(2,1)S(1)}, u32[]{:S(2)}, u32[]{:S(2)}) collective-permute-start(bf16[2304,256]{1,0:T(8,128)(2,1)} %bitcast.17), channel_id=1, source_target_pairs={{0,16},{1,49},{16,32},{17,1},{32,48},{33,17},{48,0},{49,33},{2,18}... | collective-permute-start | bytes 3538952 | tf_op jit(solution)/shard_map/ppermute | solution.py:340
  19.5 11.7 %collective-permute-start.8 = (bf16[1152,256]{1,0:T(8,128)(2,1)S(1)}, bf16[1152,256]{1,0:T(8,128)(2,1)}, u32[]{:S(2)}, u32[]{:S(2)}) collective-permute-start(bf16[1152,256]{1,0:T(8,128)(2,1)S(1)} %constant_dynamic-slice_fusion), channel_id=1, source_target_pairs={{0,16},{1,49},{16,32},{17,1},{32,48},{33,17},{48,0},{49,33},{2,18}... | collective-permute-start | bytes 1769480 | tf_op jit(solution)/shard_map/ppermute | solution.py:342
  24.4 44.6 %collective-permute-start.7 = (bf16[2304,256]{1,0:T(8,128)(2,1)S(1)}, bf16[2304,256]{1,0:T(8,128)(2,1)S(1)}, u32[]{:S(2)}, u32[]{:S(2)}) collective-permute-start(bf16[2304,256]{1,0:T(8,128)(2,1)S(1)} %collective-permute-done.6.near_mine), channel_id=1, source_target_pairs={{0,1},{1,0},{2,3},{3,2},{4,5},{5,4},{6,7},{7,6},{8,9},{9,8},{10,11... | collective-permute-start | bytes 3538952 | tf_op jit(solution)/shard_map/ppermute | solution.py:343
  31.2 37.8 %collective-permute-start.9 = (bf16[1152,256]{1,0:T(8,128)(2,1)}, bf16[1152,256]{1,0:T(8,128)(2,1)}, u32[]{:S(2)}, u32[]{:S(2)}) collective-permute-start(bf16[1152,256]{1,0:T(8,128)(2,1)} %collective-permute-done.8.far_mine), channel_id=1, source_target_pairs={{0,1},{1,0},{2,3},{3,2},{4,5},{5,4},{6,7},{7,6},{8,9},{9,8},{10,11... | collective-permute-start | bytes 1769480 | tf_op jit(solution)/shard_map/ppermute | solution.py:344
  45.1 8.7 %collective-permute-start = (bf16[80,256]{1,0:T(8,128)(2,1)}, bf16[80,256]{1,0:T(8,128)(2,1)S(1)}, u32[]{:S(2)}, u32[]{:S(2)}) collective-permute-start(bf16[80,256]{1,0:T(8,128)(2,1)} %get-tuple-element.17), channel_id=1, source_target_pairs={{0,3},{1,4},{2,5},{3,6},{4,7},{5,8},{6,9},{7,10},{8,11},{9,12},{10... | collective-permute-start | bytes 122888 | tf_op jit(solution)/shard_map/ppermute | solution.py:350
  47.0 9.9 %collective-permute-start.1 = (bf16[144,256]{1,0:T(8,128)(2,1)}, bf16[144,256]{1,0:T(8,128)(2,1)S(1)}, u32[]{:S(2)}, u32[]{:S(2)}) collective-permute-start(bf16[144,256]{1,0:T(8,128)(2,1)} %get-tuple-element.18), channel_id=1, source_target_pairs={{0,2},{1,3},{2,4},{3,5},{4,6},{5,7},{6,8},{7,9},{8,10},{9,11},{10,... | collective-permute-start | bytes 221192 | tf_op jit(solution)/shard_map/ppermute | solution.py:350
  48.9 6.4 %collective-permute-start.5 = (bf16[80,256]{1,0:T(8,128)(2,1)}, bf16[80,256]{1,0:T(8,128)(2,1)S(1)}, u32[]{:S(2)}, u32[]{:S(2)}) collective-permute-start(bf16[80,256]{1,0:T(8,128)(2,1)} %get-tuple-element.21), channel_id=1, source_target_pairs={{0,13},{1,14},{2,15},{3,0},{4,1},{5,2},{6,3},{7,4},{8,5},{9,6},{10... | collective-permute-start | bytes 122888 | tf_op jit(solution)/shard_map/ppermute | solution.py:350
  53.8 9.4 %collective-permute-start.3 = (bf16[208,256]{1,0:T(8,128)(2,1)}, bf16[208,256]{1,0:T(8,128)(2,1)S(1)}, u32[]{:S(2)}, u32[]{:S(2)}) collective-permute-start(bf16[208,256]{1,0:T(8,128)(2,1)} %get-tuple-element.19.own), channel_id=1, source_target_pairs={{0,15},{1,0},{2,1},{3,2},{4,3},{5,4},{6,5},{7,6},{8,7},{9,8},{10,9... | collective-permute-start | bytes 319496 | tf_op jit(solution)/shard_map/ppermute | solution.py:350
  55.3 7.8 %collective-permute-start.2 = (bf16[208,256]{1,0:T(8,128)(2,1)}, bf16[208,256]{1,0:T(8,128)(2,1)S(1)}, u32[]{:S(2)}, u32[]{:S(2)}) collective-permute-start(bf16[208,256]{1,0:T(8,128)(2,1)} %get-tuple-element.19.own), channel_id=1, source_target_pairs={{0,1},{1,2},{2,3},{3,4},{4,5},{5,6},{6,7},{7,8},{8,9},{9,10},{10,1... | collective-permute-start | bytes 319496 | tf_op jit(solution)/shard_map/ppermute | solution.py:350
  56.9 6.2 %collective-permute-start.4 = (bf16[144,256]{1,0:T(8,128)(2,1)}, bf16[144,256]{1,0:T(8,128)(2,1)S(1)}, u32[]{:S(2)}, u32[]{:S(2)}) collective-permute-start(bf16[144,256]{1,0:T(8,128)(2,1)} %get-tuple-element.20), channel_id=1, source_target_pairs={{0,14},{1,15},{2,0},{3,1},{4,2},{5,3},{6,4},{7,5},{8,6},{9,7},{10,... | collective-permute-start | bytes 221192 | tf_op jit(solution)/shard_map/ppermute | solution.py:350
  63.1 0.7 copy-start
  63.8 0.9 copy-start.3
  93.5 5.2 %collective-permute-start.10 = (bf16[4,160,256]{2,1,0:T(8,128)(2,1)S(1)}, bf16[4,160,256]{2,1,0:T(8,128)(2,1)S(1)}, u32[]{:S(2)}, u32[]{:S(2)}) collective-permute-start(bf16[4,160,256]{2,1,0:T(8,128)(2,1)S(1)} %slice.4), channel_id=1, source_target_pairs={{0,1},{1,0},{2,3},{3,2},{4,5},{5,4},{6,7},{7,6},{8,9},{9,8},{10,11... | collective-permute-start | bytes 983048 | tf_op jit(solution)/shard_map/ppermute | solution.py:357
  131.1 30.6 %copy-start.1 = (s32[3]{0:T(128)S(1)}, s32[3]{0:T(128)}, u32[]{:S(2)}) copy-start(s32[3]{0:T(128)} %pad_add_fusion.ids_ref.core_ref) | copy-start | bytes 40
  155.6 7.7 %collective-permute-start.11 = (bf16[2304,128]{1,0:T(8,128)(2,1)S(1)}, bf16[2304,128]{1,0:T(8,128)(2,1)S(1)}, u32[]{:S(2)}, u32[]{:S(2)}) collective-permute-start(bf16[2304,128]{1,0:T(8,128)(2,1)S(1)} %bitcast.14), channel_id=1, source_target_pairs={{0,1},{1,0},{2,3},{3,2},{4,5},{5,4},{6,7},{7,6},{8,9},{9,8},{10,11... | collective-permute-start | bytes 1769480 | tf_op jit(solution)/shard_map/ppermute | solution.py:377

commit v2 on v1

--- a/solution.py
+++ b/solution.py
@@ -33,9 +33,7 @@
 OFF = 16
 OWN = REACH
 HROWS, PROWS, GROWS = PIX, PIX + HALO, PIX
-FOLD = PROWS // 2
-AT_H, AT_PRE, AT_G = FOLD, FOLD + HROWS, 2 * FOLD + HROWS
-MSG = AT_G + GROWS
+MSG = HROWS + PROWS + GROWS
 
 
 def expand(gat, t, src, hot):
@@ -190,7 +188,7 @@
         der[level, lo:hi, :] = 1.0 - squash * squash
         if level + 1 < LEVELS:
             h_buf[level, PAD + lo:PAD + hi, :] = (src[PAD + lo:PAD + hi, :].astype(F32) + squash).astype(BF)
-        out_ref[level, AT_H:AT_PRE, :] = src[PAD + OWN:PAD + OWN + PIX, :]
+        out_ref[level, :HROWS, :] = src[PAD + OWN:PAD + OWN + PIX, :]
 
     for level in range(LEVELS - 1, -1, -1):
         lo, hi = PRE_ROWS[level]
@@ -207,29 +205,24 @@
                                             preferred_element_type=F32)
         g_buf[PAD + lo:PAD + hi, :] = total.astype(BF)
         start = pl.multiple_of(PAD + OWN - HALO + HALO * core, HALO)
-        for at, half in ((0, 1 - core), (AT_PRE, core)):
-            part = pre_buf[pl.ds(start, PROWS), pl.ds(pl.multiple_of(half * 128, 128), 128)]
-            out_ref[level, at:at + FOLD, :128] = part[:FOLD]
-            out_ref[level, at:at + FOLD, 128:] = part[FOLD:]
-        out_ref[level, AT_G:, :] = g_buf[PAD + OWN:PAD + OWN + PIX, :]
+        out_ref[level, HROWS:HROWS + PROWS, :] = pre_buf[pl.ds(start, PROWS), :]
+        out_ref[level, HROWS + PROWS:, :] = g_buf[PAD + OWN:PAD + OWN + PIX, :]
 
 
 def grad_kernel(core_ref, mine, other, hot, out_ref, gin_ref, p_buf, h_buf, t_buf):
     core = core_ref[0]
     micro = mine.shape[0]
     pair = 2 * PIX
-    gin_ref[...] = mine[:, AT_G:, :]
+    gin_ref[...] = mine[:, HROWS + PROWS:, :]
     for c in range(2):
         @pl.when(core == c)
         def _(c=c):
-            both = ((mine, AT_PRE), (other, 0))
+            both = (mine, other) if c == 0 else (other, mine)
             for m in range(micro):
-                for n, (ref, at) in enumerate(both if c == 0 else both[::-1]):
-                    for side in range(2):
-                        to = n * PROWS + side * FOLD
-                        p_buf[to:to + FOLD, m * 128:(m + 1) * 128] = (
-                            ref[m, at:at + FOLD, side * 128:(side + 1) * 128])
-                    h_buf[m * pair + n * PIX:m * pair + (n + 1) * PIX, :] = ref[m, AT_H:AT_PRE, :]
+                for n, ref in enumerate(both):
+                    p_buf[n * PROWS:(n + 1) * PROWS, m * 128:(m + 1) * 128] = (
+                        ref[m, HROWS:HROWS + PROWS, c * 128:(c + 1) * 128])
+                    h_buf[m * pair + n * PIX:m * pair + (n + 1) * PIX, :] = ref[m, :HROWS, :]
     h_t = jnp.transpose(h_buf[...].astype(F32)).astype(BF)
     pre = p_buf[...]
     for k in range(TAPS):
@@ -354,7 +347,7 @@
     out, _ = stack_call(cores, h0, g_top, s_hot, st_hot, gat0, w_all, near_other, far, far_other)
 
     mine = lax.all_to_all(out, "section", 0, 0, tiled=True)
-    other = lax.ppermute(mine[:, :AT_PRE], "core", shift(2, 1))
+    other = lax.ppermute(mine[:, :HROWS + PROWS], "core", shift(2, 1))
     chips = lax.axis_size("dp") * lax.axis_size("py")
     rows = TAPS * C
     blocks = (chips, rows // chips // 4, 4, 128)

time: 165 us -> 165 us (level)
  no operation moved by 1% of the time
where the time goes in v2:
time: 165 us
  blocking collectives  67.2 us (41%)
  starting transfers between devices  53.5 us (32%)
  Pallas kernels  23.5 us (14%)
  waiting for transfers between devices  17.6 us (11%)
    all_to_all x1, blocking collectives, step(): lax.all_to_all(part.reshape(blocks), ('dp', 'py'), 0, 0, tiled=True)  30.6 us
    all_to_all x1, blocking collectives, step(): lax.all_to_all(total.reshape(blocks), ('dp', 'py'), 0, 0, tiled=True)  24.4 us
    ppermute x6, starting transfers between devices, step(): sends.append(send(block, perm=shift(patches, by)))  15.7 us
    ppermute x1, waiting for transfers between devices, step(): near = lax.ppermute(weights[0], ('section', 'core'), ways)  13.4 us
    all_to_all x1, blocking collectives, step(): mine = lax.all_to_all(out, 'section', 0, 0, tiled=True)  12.2 us
    pallas_call x1, Pallas kernels, stack_call(): call(stack_kernel, [jax.ShapeDtypeStruct((LEVELS, MSG, C), BF), jax.Shape...  12.2 us
    ppermute x1, starting transfers between devices, step(): far_other = lax.ppermute(far, 'core', shift(2, 1))  11 us
    ppermute x1, starting transfers between devices, step(): near_other = lax.ppermute(near, 'core', shift(2, 1))  6.61 us
  transfers between devices with their start and end apart: 12, of which 6 were waited for; matrix products, arithmetic and copies ran while one was open for 0% of the time, Pallas kernels for 5%

profile of v2, /device:TPU:1, one launch (start us, length us, event | category | flops | bytes accessed | tf_op | source)
XLA Modules:
  0.0 164.8 jit_solution(14316367516318567301)
XLA Ops:
  0.6 5.3 %collective-permute-start.6 = (bf16[2304,256]{1,0:T(8,128)(2,1)}, bf16[2304,256]{1,0:T(8,128)(2,1)S(1)}, u32[]{:S(2)}, u32[]{:S(2)}) collective-permute-start(bf16[2304,256]{1,0:T(8,128)(2,1)} %bitcast.17), channel_id=1, source_target_pairs={{0,16},{1,49},{16,32},{17,1},{32,48},{33,17},{48,0},{49,33},{2,18}... | collective-permute-start | bytes 3538952 | tf_op jit(solution)/shard_map/ppermute | solution.py:333
  6.0 13.4 %collective-permute-done.6.near_mine = bf16[2304,256]{1,0:T(8,128)(2,1)S(1)} collective-permute-done((bf16[2304,256]{1,0:T(8,128)(2,1)}, bf16[2304,256]{1,0:T(8,128)(2,1)S(1)}, u32[]{:S(2)}, u32[]{:S(2)}) %collective-permute-start.6) | collective-permute-done | bytes 1179680 | tf_op jit(solution)/shard_map/ppermute | solution.py:333
  19.5 4.9 %collective-permute-start.8 = (bf16[1152,256]{1,0:T(8,128)(2,1)S(1)}, bf16[1152,256]{1,0:T(8,128)(2,1)}, u32[]{:S(2)}, u32[]{:S(2)}) collective-permute-start(bf16[1152,256]{1,0:T(8,128)(2,1)S(1)} %constant_dynamic-slice_fusion), channel_id=1, source_target_pairs={{0,16},{1,49},{16,32},{17,1},{32,48},{33,17},{48,0},{49,33},{2,18}... | collective-permute-start | bytes 1769480 | tf_op jit(solution)/shard_map/ppermute | solution.py:335
  24.4 6.6 %collective-permute-start.7 = (bf16[2304,256]{1,0:T(8,128)(2,1)S(1)}, bf16[2304,256]{1,0:T(8,128)(2,1)S(1)}, u32[]{:S(2)}, u32[]{:S(2)}) collective-permute-start(bf16[2304,256]{1,0:T(8,128)(2,1)S(1)} %collective-permute-done.6.near_mine), channel_id=1, source_target_pairs={{0,1},{1,0},{2,3},{3,2},{4,5},{5,4},{6,7},{7,6},{8,9},{9,8},{10,11... | collective-permute-start | bytes 3538952 | tf_op jit(solution)/shard_map/ppermute | solution.py:336
  31.2 11.0 %collective-permute-start.9 = (bf16[1152,256]{1,0:T(8,128)(2,1)}, bf16[1152,256]{1,0:T(8,128)(2,1)}, u32[]{:S(2)}, u32[]{:S(2)}) collective-permute-start(bf16[1152,256]{1,0:T(8,128)(2,1)} %collective-permute-done.8.far_mine), channel_id=1, source_target_pairs={{0,1},{1,0},{2,3},{3,2},{4,5},{5,4},{6,7},{7,6},{8,9},{9,8},{10,11... | collective-permute-start | bytes 1769480 | tf_op jit(solution)/shard_map/ppermute | solution.py:337
  42.8 2.2 %shard_map.59 = (bf16[208,256]{1,0:T(8,128)(2,1)}, bf16[144,256]{1,0:T(8,128)(2,1)}, bf16[144,256]{1,0:T(8,128)(2,1)}, bf16[80,256]{1,0:T(8,128)(2,1)}, bf16[80,256]{1,0:T(8,128)(2,1)}) custom-call(s32[3]{0:T(128)} %pad_add_fusion.ids_ref.core_ref, bf16[4,1,96,256]{3,2,1,0:T(8,128)(2,1)} %maps.1, bf16[4,1,96,256]{3,2,1,0:T(8,128)(2,1)} %upstream.1, ...), custom_call_target="tpu_custom_call" | custom-call | bytes 1000000 | tf_op jit(solution)/shard_map/pallas_call | solution.py:84
  45.1 1.9 %collective-permute-start = (bf16[80,256]{1,0:T(8,128)(2,1)}, bf16[80,256]{1,0:T(8,128)(2,1)S(1)}, u32[]{:S(2)}, u32[]{:S(2)}) collective-permute-start(bf16[80,256]{1,0:T(8,128)(2,1)} %get-tuple-element.17), channel_id=1, source_target_pairs={{0,3},{1,4},{2,5},{3,6},{4,7},{5,8},{6,9},{7,10},{8,11},{9,12},{10... | collective-permute-start | bytes 122888 | tf_op jit(solution)/shard_map/ppermute | solution.py:343
  47.0 1.9 %collective-permute-start.1 = (bf16[144,256]{1,0:T(8,128)(2,1)}, bf16[144,256]{1,0:T(8,128)(2,1)S(1)}, u32[]{:S(2)}, u32[]{:S(2)}) collective-permute-start(bf16[144,256]{1,0:T(8,128)(2,1)} %get-tuple-element.18), channel_id=1, source_target_pairs={{0,2},{1,3},{2,4},{3,5},{4,6},{5,7},{6,8},{7,9},{8,10},{9,11},{10,... | collective-permute-start | bytes 221192 | tf_op jit(solution)/shard_map/ppermute | solution.py:343
  48.9 4.9 %collective-permute-start.5 = (bf16[80,256]{1,0:T(8,128)(2,1)}, bf16[80,256]{1,0:T(8,128)(2,1)S(1)}, u32[]{:S(2)}, u32[]{:S(2)}) collective-permute-start(bf16[80,256]{1,0:T(8,128)(2,1)} %get-tuple-element.21), channel_id=1, source_target_pairs={{0,13},{1,14},{2,15},{3,0},{4,1},{5,2},{6,3},{7,4},{8,5},{9,6},{10... | collective-permute-start | bytes 122888 | tf_op jit(solution)/shard_map/ppermute | solution.py:343
  53.8 0.9 collective-permute-start.3
  55.3 1.6 collective-permute-start.2
  56.9 4.5 %collective-permute-start.4 = (bf16[144,256]{1,0:T(8,128)(2,1)}, bf16[144,256]{1,0:T(8,128)(2,1)S(1)}, u32[]{:S(2)}, u32[]{:S(2)}) collective-permute-start(bf16[144,256]{1,0:T(8,128)(2,1)} %get-tuple-element.20), channel_id=1, source_target_pairs={{0,14},{1,15},{2,0},{3,1},{4,2},{5,3},{6,4},{7,5},{8,6},{9,7},{10,... | collective-permute-start | bytes 221192 | tf_op jit(solution)/shard_map/ppermute | solution.py:343
  61.4 1.7 %collective-permute-done.4.m2b = bf16[144,256]{1,0:T(8,128)(2,1)S(1)} collective-permute-done((bf16[144,256]{1,0:T(8,128)(2,1)}, bf16[144,256]{1,0:T(8,128)(2,1)S(1)}, u32[]{:S(2)}, u32[]{:S(2)}) %collective-permute-start.4) | collective-permute-done | bytes 73760 | tf_op jit(solution)/shard_map/ppermute | solution.py:343
  64.7 4.3 %shard_map.60 = (bf16[672,256]{1,0:T(8,128)(2,1)S(1)}, bf16[672,256]{1,0:T(8,128)(2,1)S(1)}, bf16[9,512,128]{2,1,0:T(8,128)(2,1)S(1)}, bf16[7,512,128]{2,1,0:T(8...) custom-call(s32[3]{0:T(128)S(1)} %copy-done, ...), custom_call_target="tpu_custom_call" | custom-call | flops 1000000000 | bytes 12000000 | tf_op jit(solution)/shard_map/pallas_call | solution.py:284
  69.0 12.2 %shard_map.61 = (bf16[4,320,256]{2,1,0:T(8,128)(2,1)S(1)}, bf16[4,2304,256]{2,1,0:T(8,128)(2,1)S(1)}) custom-call(s32[3]{0:T(128)S(1)} %copy-done, bf16[672,256]{1,0:T(8,128)(2,1)S(1)} %get-tuple-element.22.h0, bf16[672,256]{1,0:T(8,128)(2,1)S(1)} %get-tuple-element.23.g_top, ...), custom_call_target="tpu_custom_call", output_to_operand_aliasing={{1}: (6, {})} | custom-call | flops 5000000000 | bytes 10000000 | tf_op jit(solution)/shard_map/pallas_call | solution.py:303
  81.2 12.2 %all_to_all.15.mine = bf16[4,320,256]{2,1,0:T(8,128)(2,1)S(1)} all-to-all(bf16[4,320,256]{2,1,0:T(8,128)(2,1)S(1)} %get-tuple-element.28), channel_id=1, replica_groups=mesh['dp'=8,'section'=4,'py'=8,'core'=2] {'section'}, dimensions={0} | all-to-all | bytes 1310720 | tf_op jit(solution)/shard_map/all_to_all | solution.py:349
  93.5 3.9 %collective-permute-start.10 = (bf16[4,224,256]{2,1,0:T(8,128)(2,1)S(1)}, bf16[4,224,256]{2,1,0:T(8,128)(2,1)S(1)}, u32[]{:S(2)}, u32[]{:S(2)}) collective-permute-start(bf16[4,224,256]{2,1,0:T(8,128)(2,1)S(1)} %slice.4), channel_id=1, source_target_pairs={{0,1},{1,0},{2,3},{3,2},{4,5},{5,4},{6,7},{7,6},{8,9},{9,8},{10,11... | collective-permute-start | bytes 1376264 | tf_op jit(solution)/shard_map/ppermute | solution.py:350
  97.4 1.4 collective-permute-done.10.other
  98.9 1.9 %shard_map.62 = (bf16[2304,128]{1,0:T(8,128)(2,1)S(1)}, bf16[4,96,256]{2,1,0:T(8,128)(2,1)}) custom-call(s32[3]{0:T(128)S(1)} %copy-done, bf16[4,320,256]{2,1,0:T(8,128)(2,1)S(1)} %all_to_all.15.mine, bf16[4,224,256]{2,1,0:T(8,128)(2,1)S(1)} %collective-permute-done.10.other, bf16[8,192,256]{2,1,0:T(8,128)(2,1)S(1)} %get-tuple-element.29.hot), custom_call_target="tpu_custom_call" | custom-call | flops 1000000000 | bytes 2000000 | tf_op jit(solution)/shard_map/pallas_call | solution.py:354
  100.7 30.6 %all_to_all.16 = bf16[64,9,4,128]{3,2,1,0:T(4,128)(2,1)S(1)} all-to-all(bf16[64,9,4,128]{3,2,1,0:T(4,128)(2,1)S(1)} %bitcast.16), channel_id=1, replica_groups=mesh['dp'=8,'section'=4,'py'=8,'core'=2] {'dp','py'}, dimensions={0} | all-to-all | bytes 1179648 | tf_op jit(solution)/shard_map/all_to_all | solution.py:365
  131.4 24.4 %all_to_all.17 = bf16[64,9,4,128]{3,2,1,0:T(4,128)(2,1)S(1)} all-to-all(bf16[64,9,4,128]{3,2,1,0:T(4,128)(2,1)S(1)} %bitcast.13), channel_id=1, replica_groups=mesh['dp'=8,'section'=4,'py'=8,'core'=2] {'dp','py'}, dimensions={0} | all-to-all | bytes 1179648 | tf_op jit(solution)/shard_map/all_to_all | solution.py:369
  155.8 6.0 %collective-permute-start.11 = (bf16[2304,128]{1,0:T(8,128)(2,1)S(1)}, bf16[2304,128]{1,0:T(8,128)(2,1)S(1)}, u32[]{:S(2)}, u32[]{:S(2)}) collective-permute-start(bf16[2304,128]{1,0:T(8,128)(2,1)S(1)} %bitcast.14), channel_id=1, source_target_pairs={{0,1},{1,0},{2,3},{3,2},{4,5},{5,4},{6,7},{7,6},{8,9},{9,8},{10,11... | collective-permute-start | bytes 1769480 | tf_op jit(solution)/shard_map/ppermute | solution.py:370
  161.9 1.4 shard_map.64.refs_0_
  163.5 1.4 shard_map.65
  (21 shorter events, 3.5 us)
Async XLA Ops:
  0.6 62.5 %copy-start.2 = (bf16[1,2304,256]{2,1,0:T(8,128)(2,1)S(1)}, bf16[1,2304,256]{2,1,0:T(8,128)(2,1)}, u32[]{:S(2)}) copy-start(bf16[1,2304,256]{2,1,0:T(8,128)(2,1)} %param.6) | copy-start | bytes 3538948
  0.6 18.8 %collective-permute-start.6 = (bf16[2304,256]{1,0:T(8,128)(2,1)}, bf16[2304,256]{1,0:T(8,128)(2,1)S(1)}, u32[]{:S(2)}, u32[]{:S(2)}) collective-permute-start(bf16[2304,256]{1,0:T(8,128)(2,1)} %bitcast.17), channel_id=1, source_target_pairs={{0,16},{1,49},{16,32},{17,1},{32,48},{33,17},{48,0},{49,33},{2,18}... | collective-permute-start | bytes 3538952 | tf_op jit(solution)/shard_map/ppermute | solution.py:333
  19.5 11.7 %collective-permute-start.8 = (bf16[1152,256]{1,0:T(8,128)(2,1)S(1)}, bf16[1152,256]{1,0:T(8,128)(2,1)}, u32[]{:S(2)}, u32[]{:S(2)}) collective-permute-start(bf16[1152,256]{1,0:T(8,128)(2,1)S(1)} %constant_dynamic-slice_fusion), channel_id=1, source_target_pairs={{0,16},{1,49},{16,32},{17,1},{32,48},{33,17},{48,0},{49,33},{2,18}... | collective-permute-start | bytes 1769480 | tf_op jit(solution)/shard_map/ppermute | solution.py:335
  24.4 44.6 %collective-permute-start.7 = (bf16[2304,256]{1,0:T(8,128)(2,1)S(1)}, bf16[2304,256]{1,0:T(8,128)(2,1)S(1)}, u32[]{:S(2)}, u32[]{:S(2)}) collective-permute-start(bf16[2304,256]{1,0:T(8,128)(2,1)S(1)} %collective-permute-done.6.near_mine), channel_id=1, source_target_pairs={{0,1},{1,0},{2,3},{3,2},{4,5},{5,4},{6,7},{7,6},{8,9},{9,8},{10,11... | collective-permute-start | bytes 3538952 | tf_op jit(solution)/shard_map/ppermute | solution.py:336
  31.2 37.8 %collective-permute-start.9 = (bf16[1152,256]{1,0:T(8,128)(2,1)}, bf16[1152,256]{1,0:T(8,128)(2,1)}, u32[]{:S(2)}, u32[]{:S(2)}) collective-permute-start(bf16[1152,256]{1,0:T(8,128)(2,1)} %collective-permute-done.8.far_mine), channel_id=1, source_target_pairs={{0,1},{1,0},{2,3},{3,2},{4,5},{5,4},{6,7},{7,6},{8,9},{9,8},{10,11... | collective-permute-start | bytes 1769480 | tf_op jit(solution)/shard_map/ppermute | solution.py:337
  45.1 8.7 %collective-permute-start = (bf16[80,256]{1,0:T(8,128)(2,1)}, bf16[80,256]{1,0:T(8,128)(2,1)S(1)}, u32[]{:S(2)}, u32[]{:S(2)}) collective-permute-start(bf16[80,256]{1,0:T(8,128)(2,1)} %get-tuple-element.17), channel_id=1, source_target_pairs={{0,3},{1,4},{2,5},{3,6},{4,7},{5,8},{6,9},{7,10},{8,11},{9,12},{10... | collective-permute-start | bytes 122888 | tf_op jit(solution)/shard_map/ppermute | solution.py:343
  47.0 9.9 %collective-permute-start.1 = (bf16[144,256]{1,0:T(8,128)(2,1)}, bf16[144,256]{1,0:T(8,128)(2,1)S(1)}, u32[]{:S(2)}, u32[]{:S(2)}) collective-permute-start(bf16[144,256]{1,0:T(8,128)(2,1)} %get-tuple-element.18), channel_id=1, source_target_pairs={{0,2},{1,3},{2,4},{3,5},{4,6},{5,7},{6,8},{7,9},{8,10},{9,11},{10,... | collective-permute-start | bytes 221192 | tf_op jit(solution)/shard_map/ppermute | solution.py:343
  48.9 6.4 %collective-permute-start.5 = (bf16[80,256]{1,0:T(8,128)(2,1)}, bf16[80,256]{1,0:T(8,128)(2,1)S(1)}, u32[]{:S(2)}, u32[]{:S(2)}) collective-permute-start(bf16[80,256]{1,0:T(8,128)(2,1)} %get-tuple-element.21), channel_id=1, source_target_pairs={{0,13},{1,14},{2,15},{3,0},{4,1},{5,2},{6,3},{7,4},{8,5},{9,6},{10... | collective-permute-start | bytes 122888 | tf_op jit(solution)/shard_map/ppermute | solution.py:343
  53.8 9.4 %collective-permute-start.3 = (bf16[208,256]{1,0:T(8,128)(2,1)}, bf16[208,256]{1,0:T(8,128)(2,1)S(1)}, u32[]{:S(2)}, u32[]{:S(2)}) collective-permute-start(bf16[208,256]{1,0:T(8,128)(2,1)} %get-tuple-element.19.own), channel_id=1, source_target_pairs={{0,15},{1,0},{2,1},{3,2},{4,3},{5,4},{6,5},{7,6},{8,7},{9,8},{10,9... | collective-permute-start | bytes 319496 | tf_op jit(solution)/shard_map/ppermute | solution.py:343
  55.3 7.8 %collective-permute-start.2 = (bf16[208,256]{1,0:T(8,128)(2,1)}, bf16[208,256]{1,0:T(8,128)(2,1)S(1)}, u32[]{:S(2)}, u32[]{:S(2)}) collective-permute-start(bf16[208,256]{1,0:T(8,128)(2,1)} %get-tuple-element.19.own), channel_id=1, source_target_pairs={{0,1},{1,2},{2,3},{3,4},{4,5},{5,6},{6,7},{7,8},{8,9},{9,10},{10,1... | collective-permute-start | bytes 319496 | tf_op jit(solution)/shard_map/ppermute | solution.py:343
  56.9 6.2 %collective-permute-start.4 = (bf16[144,256]{1,0:T(8,128)(2,1)}, bf16[144,256]{1,0:T(8,128)(2,1)S(1)}, u32[]{:S(2)}, u32[]{:S(2)}) collective-permute-start(bf16[144,256]{1,0:T(8,128)(2,1)} %get-tuple-element.20), channel_id=1, source_target_pairs={{0,14},{1,15},{2,0},{3,1},{4,2},{5,3},{6,4},{7,5},{8,6},{9,7},{10,... | collective-permute-start | bytes 221192 | tf_op jit(solution)/shard_map/ppermute | solution.py:343
  63.1 0.7 copy-start
  63.8 0.9 copy-start.3
  93.5 5.4 %collective-permute-start.10 = (bf16[4,224,256]{2,1,0:T(8,128)(2,1)S(1)}, bf16[4,224,256]{2,1,0:T(8,128)(2,1)S(1)}, u32[]{:S(2)}, u32[]{:S(2)}) collective-permute-start(bf16[4,224,256]{2,1,0:T(8,128)(2,1)S(1)} %slice.4), channel_id=1, source_target_pairs={{0,1},{1,0},{2,3},{3,2},{4,5},{5,4},{6,7},{7,6},{8,9},{9,8},{10,11... | collective-permute-start | bytes 1376264 | tf_op jit(solution)/shard_map/ppermute | solution.py:350
  131.3 30.6 %copy-start.1 = (s32[3]{0:T(128)S(1)}, s32[3]{0:T(128)}, u32[]{:S(2)}) copy-start(s32[3]{0:T(128)} %pad_add_fusion.ids_ref.core_ref) | copy-start | bytes 40
  155.8 7.7 %collective-permute-start.11 = (bf16[2304,128]{1,0:T(8,128)(2,1)S(1)}, bf16[2304,128]{1,0:T(8,128)(2,1)S(1)}, u32[]{:S(2)}, u32[]{:S(2)}) collective-permute-start(bf16[2304,128]{1,0:T(8,128)(2,1)S(1)} %bitcast.14), channel_id=1, source_target_pairs={{0,1},{1,0},{2,3},{3,2},{4,5},{5,4},{6,7},{7,6},{8,9},{9,8},{10,11... | collective-permute-start | bytes 1769480 | tf_op jit(solution)/shard_map/ppermute | solution.py:370
